TPU v7x, 512 devices: a whole 4x8x8 slice. The times are simulated.
512 devices in a mesh: space: 64 (over y, z), orb: 8 (over x, core).
Axes of the slice: x: 4, y: 8, z: 8, core: 2. Of those that a mesh axis runs over, the one named last changes fastest.
Arguments:
- hamiltonian: bfloat16 [512, 7, 256, 256], P('space'), may hold values from -0.125 to 0.125
- orbitals: bfloat16 [256, 131072], P('orb', 'space'), may hold values from -6 to 6
- adjacency: int32 [512, 6], P('space'), may hold values from 0 to 511, as said below
Outputs:
- basis: float32 [256, 131072], P('orb', 'space')
- factor: float32 [256, 256], replicated
Inputs may be any that keep to these rules, and one draw needn't show every extreme that they name: `adjacency`: with elements in blocks of 8 (block b holds elements b * 8 to b * 8 + 7), face 0 of an element in block b lies in block b - 1 and face 1 in block b + 1 (both modulo the number of blocks), faces 2 to 5 in block b; for each face, the elements of a block name every element of the target block exactly once.
All inputs are finite; a program needn't handle non-finite values.
Results may differ from a plain program's by a relative error of at most 0.0041.
Values may be sent and summed in bfloat16 or wider, within the bound.
A program may use at most 64 MiB of HBM per device.

v0:
```python
import jax
import jax.numpy as jnp
from jax import lax
from jax.sharding import PartitionSpec as P

centre = 0.25
radius = 0.75


def with_halo(block, sides, width):
    for axis, dim in sides:
        count = lax.axis_size(axis)
        forward = [(i, i + 1) for i in range(count - 1)]
        forward.append((count - 1, 0))
        backward = [(target, source) for source, target in forward]
        low = lax.ppermute(
            lax.slice_in_dim(block, block.shape[dim] - width, None, axis=dim), axis, forward
        )
        high = lax.ppermute(lax.slice_in_dim(block, 0, width, axis=dim), axis, backward)
        block = jnp.concatenate([low, block, high], axis=dim)
    return block


def shards(hamiltonian, orbitals, adjacency):
    count = hamiltonian.shape[0]
    width = hamiltonian.shape[2]
    owned = orbitals.shape[0]
    total = count * lax.axis_size("space")
    first = lax.axis_index("space") * count
    located = (adjacency - first + count) % total

    def apply_ham(vec):
        padded = with_halo(vec, (("space", 1),), count * width)
        blocks = padded.reshape(owned, 3 * count, width)
        near = jnp.take(blocks, located.reshape(-1), axis=1).reshape(owned, count, 6, width)
        own_part = vec.reshape(owned, count, width)
        result = jnp.einsum(
            "oej,eij->oei", own_part, hamiltonian[:, 0], preferred_element_type=jnp.float32
        )
        result = result + jnp.einsum(
            "oefj,efij->oei", near, hamiltonian[:, 1:], preferred_element_type=jnp.float32
        )
        return result.reshape(owned, count * width)

    level_zero = orbitals.astype(jnp.float32)
    level_one = ((apply_ham(orbitals) - centre * level_zero) / radius).astype(jnp.bfloat16)
    one_wide = level_one.astype(jnp.float32)
    level_two = (2.0 * (apply_ham(level_one) - centre * one_wide) / radius - level_zero).astype(
        jnp.bfloat16
    )
    two_wide = level_two.astype(jnp.float32)
    filtered = 2.0 * (apply_ham(level_two) - centre * two_wide) / radius - one_wide
    row_piece = lax.all_to_all(filtered, "orb", split_axis=1, concat_axis=0, tiled=True)
    partial_gram = jnp.dot(row_piece, row_piece.T, precision=lax.Precision.HIGHEST)
    gram = lax.psum(partial_gram, ("space", "orb"))
    lower = jnp.linalg.cholesky(gram)
    solved = lax.linalg.triangular_solve(lower, row_piece, left_side=True, lower=True)
    basis = lax.all_to_all(solved, "orb", split_axis=0, concat_axis=1, tiled=True)
    return (basis, lower.T)


def solution(mesh):
    in_specs = (P("space", None, None, None), P("orb", "space"), P("space", None))
    out_specs = (P("orb", "space"), P())
    return jax.shard_map(shards, mesh=mesh, in_specs=in_specs, out_specs=out_specs, check_vma=False)
```

profile of v0, /device:TPU:24, one launch (start us, length us, event | category | flops | bytes accessed | tf_op | source)
XLA Modules:
  0.0 435.6 jit_solution(6208198198700955853)
XLA Ops:
  7.2 4.4 %collective-permute-start = (bf16[32,2048]{1,0:T(8,128)(2,1)}, bf16[32,2048]{1,0:T(8,128)(2,1)S(1)}, u32[]{:S(2)}, u32[]{:S(2)}) collective-permute-start(bf16[32,2048]{1,0:T(8,128)(2,1)} %param.6), channel_id=1, source_target_pairs={{0,8},{8,16},{16,24},{24,32},{32,40},{40,48},{48,56},{56,64},{64,7... | collective-permute-start | bytes 393224 | tf_op jit(solution)/shard_map/ppermute | solution.py:16
  11.6 8.5 %collective-permute-start.1 = (bf16[32,2048]{1,0:T(8,128)(2,1)}, bf16[32,2048]{1,0:T(8,128)(2,1)S(1)}, u32[]{:S(2)}, u32[]{:S(2)}) collective-permute-start(bf16[32,2048]{1,0:T(8,128)(2,1)} %param.6), channel_id=1, source_target_pairs={{8,0},{16,8},{24,16},{32,24},{40,32},{48,40},{56,48},{64,56},{72,6... | collective-permute-start | bytes 393224 | tf_op jit(solution)/shard_map/ppermute | solution.py:19
  21.8 1.3 collective-permute-done.1
  24.9 4.7 %fusion.6 = f32[32,8,256]{2,0,1:T(8,128)S(1)} fusion(bf16[32,8,6,256]{3,0,2,1:T(8,128)(2,1)S(1)} %bitcast.139, bf16[8,7,256,256]{3,2,1,0:T(8,128)(2,1)} %param.5), kind=kOutput, calls=%fused_computation.11 | convolution fusion | flops 201326592 | bytes 7340032 | tf_op jit(solution)/shard_map/oefj,efij->oei/dot_general | solution.py:40
  29.6 1.6 fusion.16
  31.3 1.9 collective-permute-start.2
  33.3 6.4 %collective-permute-start.3 = (bf16[32,2048]{1,0:T(8,128)(2,1)S(1)}, bf16[32,2048]{1,0:T(8,128)(2,1)S(1)}, u32[]{:S(2)}, u32[]{:S(2)}) collective-permute-start(bf16[32,2048]{1,0:T(8,128)(2,1)S(1)} %fusion.27), channel_id=1, source_target_pairs={{8,0},{16,8},{24,16},{32,24},{40,32},{48,40},{56,48},{64,56},{72,6... | collective-permute-start | bytes 393224 | tf_op jit(solution)/shard_map/ppermute | solution.py:19
  39.7 1.0 collective-permute-done.2
  40.7 1.5 collective-permute-done.3
  43.0 4.7 %fusion.9 = f32[8,32,256]{2,1,0:T(8,128)S(1)} fusion(bf16[32,8,6,256]{3,0,2,1:T(8,128)(2,1)S(1)} %bitcast.140, bf16[8,7,256,256]{3,2,1,0:T(8,128)(2,1)} %param.5), kind=kOutput, calls=%fused_computation.12 | convolution fusion | flops 201326592 | bytes 7340032 | tf_op jit(solution)/shard_map/oefj,efij->oei/dot_general | solution.py:40
  47.7 1.7 fusion.18
  49.5 2.9 collective-permute-start.4
  52.4 5.5 %collective-permute-start.5 = (bf16[32,2048]{1,0:T(8,128)(2,1)S(1)}, bf16[32,2048]{1,0:T(8,128)(2,1)S(1)}, u32[]{:S(2)}, u32[]{:S(2)}) collective-permute-start(bf16[32,2048]{1,0:T(8,128)(2,1)S(1)} %fusion.28), channel_id=1, source_target_pairs={{8,0},{16,8},{24,16},{32,24},{40,32},{48,40},{56,48},{64,56},{72,6... | collective-permute-start | bytes 393224 | tf_op jit(solution)/shard_map/ppermute | solution.py:19
  57.9 1.0 collective-permute-done.4
  58.9 1.5 collective-permute-done.5
  61.2 4.7 %fusion.12 = f32[8,32,256]{2,1,0:T(8,128)S(1)} fusion(bf16[32,8,6,256]{3,0,2,1:T(8,128)(2,1)S(1)} %bitcast.138, bf16[8,7,256,256]{3,2,1,0:T(8,128)(2,1)} %param.5), kind=kOutput, calls=%fused_computation.13 | convolution fusion | flops 201326592 | bytes 7340032 | tf_op jit(solution)/shard_map/oefj,efij->oei/dot_general | solution.py:40
  65.9 1.7 fusion.17
  68.4 4.3 all-to-all-start
  73.0 7.3 %all-to-all-done = f32[32,8,256]{2,0,1:T(8,128)S(1)} async-done(((f32[32,8,256]{2,0,1:T(8,128)}), f32[32,8,256]{2,0,1:T(8,128)S(1)}, u32[]{:S(2)}, u32[]{:S(2)}) %all-to-all-start) | async-done | bytes 262176 | tf_op jit(solution)/shard_map/all_to_all | solution.py:53
  80.2 1.1 fusion.49
  81.4 271.7 %all-reduce.3.cloned.1.call-done = f32[256,256]{0,1:T(8,128)} async-done(((f32[256,256]{0,1:T(8,128)}), f32[256,256]{0,1:T(8,128)}) %all-reduce.3.cloned.1.call-update) | async-done | bytes 262160 | tf_op jit(solution)/shard_map/psum | solution.py:55
  353.1 1.1 copy.40
  354.2 1.0 fusion.31
  355.2 11.7 %cholesky.50 = f32[128,128]{1,0:T(8,128)S(1)} custom-call(f32[128,128]{1,0:T(8,128)S(1)} %cholesky.118), custom_call_target="Cholesky" | custom-call | tf_op jit(solution)/shard_map/jit(cholesky)/cholesky | solution.py:56
  366.9 9.8 %custom-call.14 = f32[1,128,128]{1,2,0:T(8,128)S(1)} custom-call(f32[1,128,128]{2,1,0:T(8,128)S(1)} %get-tuple-element.34), custom_call_target="InvertDiagBlocksLowerTriangular" | custom-call | tf_op jit(solution)/shard_map/jit(cholesky)/cholesky | solution.py:56
  377.2 11.7 %cholesky.105 = f32[128,128]{1,0:T(8,128)S(1)} custom-call(f32[128,128]{1,0:T(8,128)S(1)} %convolution_subtract_fusion.1), custom_call_target="Cholesky" | custom-call | tf_op jit(solution)/shard_map/jit(cholesky)/cholesky | solution.py:56
  391.0 4.0 while.1
  391.7 1.3 bitcast_dynamic-update-slice_fusion.2
  393.7 1.3 bitcast_dynamic-update-slice_fusion.2
  395.0 19.7 %custom-call.15 = f32[2,128,128]{1,2,0:T(8,128)S(1)} custom-call(f32[2,128,128]{2,1,0:T(8,128)S(1)} %get-tuple-element.10), custom_call_target="InvertDiagBlocksLowerTriangular" | custom-call | tf_op jit(solution)/shard_map/triangular_solve | solution.py:57
  416.3 4.3 all-to-all-start.1
  421.4 6.7 %all-to-all-done.1 = f32[8,32,256]{2,1,0:T(8,128)S(1)} async-done(((f32[8,32,256]{2,1,0:T(8,128)}), f32[8,32,256]{2,1,0:T(8,128)S(1)}, u32[]{:S(2)}, u32[]{:S(2)}) %all-to-all-start.1) | async-done | bytes 262176 | tf_op jit(solution)/shard_map/all_to_all | solution.py:58
  (51 shorter events, 12.1 us)
Async XLA Ops:
  7.2 22.4 %copy-start = (bf16[32,2048]{1,0:T(8,128)(2,1)S(1)}, bf16[32,2048]{1,0:T(8,128)(2,1)}, u32[]{:S(2)}) copy-start(bf16[32,2048]{1,0:T(8,128)(2,1)} %param.6) | copy-start | bytes 393220
  7.2 14.7 %collective-permute-start = (bf16[32,2048]{1,0:T(8,128)(2,1)}, bf16[32,2048]{1,0:T(8,128)(2,1)S(1)}, u32[]{:S(2)}, u32[]{:S(2)}) collective-permute-start(bf16[32,2048]{1,0:T(8,128)(2,1)} %param.6), channel_id=1, source_target_pairs={{0,8},{8,16},{16,24},{24,32},{32,40},{40,48},{48,56},{56,64},{64,7... | collective-permute-start | bytes 393224 | tf_op jit(solution)/shard_map/ppermute | solution.py:16
  11.6 11.5 %collective-permute-start.1 = (bf16[32,2048]{1,0:T(8,128)(2,1)}, bf16[32,2048]{1,0:T(8,128)(2,1)S(1)}, u32[]{:S(2)}, u32[]{:S(2)}) collective-permute-start(bf16[32,2048]{1,0:T(8,128)(2,1)} %param.6), channel_id=1, source_target_pairs={{8,0},{16,8},{24,16},{32,24},{40,32},{48,40},{56,48},{64,56},{72,6... | collective-permute-start | bytes 393224 | tf_op jit(solution)/shard_map/ppermute | solution.py:19
  31.3 9.3 %collective-permute-start.2 = (bf16[32,2048]{1,0:T(8,128)(2,1)S(1)}, bf16[32,2048]{1,0:T(8,128)(2,1)S(1)}, u32[]{:S(2)}, u32[]{:S(2)}) collective-permute-start(bf16[32,2048]{1,0:T(8,128)(2,1)S(1)} %fusion.27), channel_id=1, source_target_pairs={{0,8},{8,16},{16,24},{24,32},{32,40},{40,48},{48,56},{56,64},{64,7... | collective-permute-start | bytes 393224 | tf_op jit(solution)/shard_map/ppermute | solution.py:16
  33.3 8.9 %collective-permute-start.3 = (bf16[32,2048]{1,0:T(8,128)(2,1)S(1)}, bf16[32,2048]{1,0:T(8,128)(2,1)S(1)}, u32[]{:S(2)}, u32[]{:S(2)}) collective-permute-start(bf16[32,2048]{1,0:T(8,128)(2,1)S(1)} %fusion.27), channel_id=1, source_target_pairs={{8,0},{16,8},{24,16},{32,24},{40,32},{48,40},{56,48},{64,56},{72,6... | collective-permute-start | bytes 393224 | tf_op jit(solution)/shard_map/ppermute | solution.py:19
  49.5 9.4 %collective-permute-start.4 = (bf16[32,2048]{1,0:T(8,128)(2,1)S(1)}, bf16[32,2048]{1,0:T(8,128)(2,1)S(1)}, u32[]{:S(2)}, u32[]{:S(2)}) collective-permute-start(bf16[32,2048]{1,0:T(8,128)(2,1)S(1)} %fusion.28), channel_id=1, source_target_pairs={{0,8},{8,16},{16,24},{24,32},{32,40},{40,48},{48,56},{56,64},{64,7... | collective-permute-start | bytes 393224 | tf_op jit(solution)/shard_map/ppermute | solution.py:16
  52.4 8.0 %collective-permute-start.5 = (bf16[32,2048]{1,0:T(8,128)(2,1)S(1)}, bf16[32,2048]{1,0:T(8,128)(2,1)S(1)}, u32[]{:S(2)}, u32[]{:S(2)}) collective-permute-start(bf16[32,2048]{1,0:T(8,128)(2,1)S(1)} %fusion.28), channel_id=1, source_target_pairs={{8,0},{16,8},{24,16},{32,24},{40,32},{48,40},{56,48},{64,56},{72,6... | collective-permute-start | bytes 393224 | tf_op jit(solution)/shard_map/ppermute | solution.py:19
  68.4 11.8 %all-to-all-start = ((f32[32,8,256]{2,0,1:T(8,128)}), f32[32,8,256]{2,0,1:T(8,128)S(1)}, u32[]{:S(2)}, u32[]{:S(2)}) async-start(f32[32,8,256]{2,0,1:T(8,128)} %bitcast.115), calls=%async_computation | async-start | bytes 524288 | tf_op jit(solution)/shard_map/all_to_all | solution.py:53
  72.7 280.4 %all-reduce.3.cloned.1.call-start = ((), (), s32[]{:S(2)}) async-start(), calls=%async_computation.2 | async-start | bytes 524288 | tf_op jit(solution)/shard_map/psum | solution.py:55
  416.3 11.8 %all-to-all-start.1 = ((f32[8,32,256]{2,1,0:T(8,128)}), f32[8,32,256]{2,1,0:T(8,128)S(1)}, u32[]{:S(2)}, u32[]{:S(2)}) async-start(f32[8,32,256]{2,1,0:T(8,128)} %bitcast.26), calls=%async_computation.1 | async-start | bytes 524288 | tf_op jit(solution)/shard_map/all_to_all | solution.py:58
Sparse Core Ops, SparseCore 0:
  81.5 271.5 all-reduce.2
where the time goes:
time: 436 us
  waiting for transfers between devices  293 us (67%)
  other arithmetic  57.7 us (13%)
  starting transfers between devices  38.4 us (9%)
  matrix products  21.5 us (5%)
  between operations  15.6 us (4%)
  local copies, waits for them, and re-layouts  9.42 us (2%)
    psum x1, waiting for transfers between devices, shards(): gram = lax.psum(partial_gram, ('space', 'orb'))  272 us
    another operation x6, other arithmetic, shards(): lower = jnp.linalg.cholesky(gram)  33.9 us
    another operation x3, other arithmetic, shards(): lax.linalg.triangular_solve(lower, row_piece, left_side=True, lower=True)  20.4 us
    ppermute x3, starting transfers between devices, with_halo(): lax.ppermute(lax.slice_in_dim(block, 0, width, axis=dim), axis, backward)  20.3 us
    dot_general x3, matrix products, apply_ham(): jnp.einsum('oefj,efij->oei', near, hamiltonian[:, 1:], preferred_element_...  14.1 us
    ppermute x3, starting transfers between devices, with_halo(): lax.ppermute(lax.slice_in_dim(block, block.shape[dim] - width, None, axis...  9.26 us
  transfers between devices with their start and end apart: 9, of which 9 were waited for; matrix products, arithmetic and copies ran while one was open for 0% of the time, Pallas kernels for 0%

commit v1 on v0

--- a/solution.py
+++ b/solution.py
@@ -52,7 +52,9 @@
     filtered = 2.0 * (apply_ham(level_two) - centre * two_wide) / radius - one_wide
     row_piece = lax.all_to_all(filtered, "orb", split_axis=1, concat_axis=0, tiled=True)
     partial_gram = jnp.dot(row_piece, row_piece.T, precision=lax.Precision.HIGHEST)
-    gram = lax.psum(partial_gram, ("space", "orb"))
+    gram = partial_gram
+    for over in ("space", "orb"):
+        gram = lax.psum(gram, over)
     lower = jnp.linalg.cholesky(gram)
     solved = lax.linalg.triangular_solve(lower, row_piece, left_side=True, lower=True)
     basis = lax.all_to_all(solved, "orb", split_axis=0, concat_axis=1, tiled=True)

time: 436 us -> 387 us (0.89)
  the two profiles are of different devices: /device:TPU:24 before, /device:TPU:1 now
where the time goes in v1:
time: 387 us; the launch traced here: 386 us
  waiting for transfers between devices  228 us (59%)
  other arithmetic  57.7 us (15%)
  starting transfers between devices  40.2 us (10%)
  matrix products  21.5 us (6%)
  between operations  15.6 us (4%)
  blocking collectives  14.1 us (4%)
  local copies, waits for them, and re-layouts  8.71 us (2%)
    psum x2, waiting for transfers between devices, shards(): gram = lax.psum(gram, over)  217 us
    another operation x6, other arithmetic, shards(): lower = jnp.linalg.cholesky(gram)  33.9 us
    ppermute x3, starting transfers between devices, with_halo(): lax.ppermute(lax.slice_in_dim(block, 0, width, axis=dim), axis, backward)  25.9 us
    another operation x3, other arithmetic, shards(): lax.linalg.triangular_solve(lower, row_piece, left_side=True, lower=True)  20.4 us
    dot_general x3, matrix products, apply_ham(): jnp.einsum('oefj,efij->oei', near, hamiltonian[:, 1:], preferred_element_...  14.1 us
    all_to_all x1, blocking collectives, shards(): lax.all_to_all(filtered, 'orb', split_axis=1, concat_axis=0, tiled=True)  14.1 us
    ppermute x3, starting transfers between devices, with_halo(): lax.ppermute(lax.slice_in_dim(block, block.shape[dim] - width, None, axis...  8.66 us
  transfers between devices with their start and end apart: 9, of which 9 were waited for; matrix products, arithmetic and copies ran while one was open for 0% of the time, Pallas kernels for 0%

profile of v1, /device:TPU:1, one launch (start us, length us, event | category | flops | bytes accessed | tf_op | source)
XLA Modules:
  0.0 385.9 jit_solution(13405184036159546715)
XLA Ops:
  7.2 4.8 %collective-permute-start = (bf16[32,2048]{1,0:T(8,128)(2,1)}, bf16[32,2048]{1,0:T(8,128)(2,1)S(1)}, u32[]{:S(2)}, u32[]{:S(2)}) collective-permute-start(bf16[32,2048]{1,0:T(8,128)(2,1)} %param.6), channel_id=1, source_target_pairs={{0,8},{8,16},{16,24},{24,32},{32,40},{40,48},{48,56},{56,64},{64,7... | collective-permute-start | bytes 393224 | tf_op jit(solution)/shard_map/ppermute | solution.py:16
  12.0 11.5 %collective-permute-start.1 = (bf16[32,2048]{1,0:T(8,128)(2,1)}, bf16[32,2048]{1,0:T(8,128)(2,1)S(1)}, u32[]{:S(2)}, u32[]{:S(2)}) collective-permute-start(bf16[32,2048]{1,0:T(8,128)(2,1)} %param.6), channel_id=1, source_target_pairs={{8,0},{16,8},{24,16},{32,24},{40,32},{48,40},{56,48},{64,56},{72,6... | collective-permute-start | bytes 393224 | tf_op jit(solution)/shard_map/ppermute | solution.py:19
  25.0 1.0 collective-permute-done.1
  26.0 0.9 pad_maximum_fusion
  27.8 4.7 %fusion.6 = f32[32,8,256]{2,0,1:T(8,128)S(1)} fusion(bf16[32,8,6,256]{3,0,2,1:T(8,128)(2,1)S(1)} %bitcast.140, bf16[8,7,256,256]{3,2,1,0:T(8,128)(2,1)} %param.5), kind=kOutput, calls=%fused_computation.11 | convolution fusion | flops 201326592 | bytes 7340032 | tf_op jit(solution)/shard_map/oefj,efij->oei/dot_general | solution.py:40
  32.5 1.6 fusion.16
  34.2 1.9 collective-permute-start.2
  36.2 7.3 %collective-permute-start.3 = (bf16[32,2048]{1,0:T(8,128)(2,1)S(1)}, bf16[32,2048]{1,0:T(8,128)(2,1)S(1)}, u32[]{:S(2)}, u32[]{:S(2)}) collective-permute-start(bf16[32,2048]{1,0:T(8,128)(2,1)S(1)} %fusion.27), channel_id=1, source_target_pairs={{8,0},{16,8},{24,16},{32,24},{40,32},{48,40},{56,48},{64,56},{72,6... | collective-permute-start | bytes 393224 | tf_op jit(solution)/shard_map/ppermute | solution.py:19
  43.9 1.5 collective-permute-done.3
  46.3 4.7 %fusion.9 = f32[8,32,256]{2,1,0:T(8,128)S(1)} fusion(bf16[32,8,6,256]{3,0,2,1:T(8,128)(2,1)S(1)} %bitcast.141, bf16[8,7,256,256]{3,2,1,0:T(8,128)(2,1)} %param.5), kind=kOutput, calls=%fused_computation.12 | convolution fusion | flops 201326592 | bytes 7340032 | tf_op jit(solution)/shard_map/oefj,efij->oei/dot_general | solution.py:40
  51.0 1.7 fusion.18
  52.7 1.9 collective-permute-start.4
  54.7 7.1 %collective-permute-start.5 = (bf16[32,2048]{1,0:T(8,128)(2,1)S(1)}, bf16[32,2048]{1,0:T(8,128)(2,1)S(1)}, u32[]{:S(2)}, u32[]{:S(2)}) collective-permute-start(bf16[32,2048]{1,0:T(8,128)(2,1)S(1)} %fusion.28), channel_id=1, source_target_pairs={{8,0},{16,8},{24,16},{32,24},{40,32},{48,40},{56,48},{64,56},{72,6... | collective-permute-start | bytes 393224 | tf_op jit(solution)/shard_map/ppermute | solution.py:19
  62.2 1.5 collective-permute-done.5
  64.6 4.7 %fusion.12 = f32[8,32,256]{2,1,0:T(8,128)S(1)} fusion(bf16[32,8,6,256]{3,0,2,1:T(8,128)(2,1)S(1)} %bitcast.139, bf16[8,7,256,256]{3,2,1,0:T(8,128)(2,1)} %param.5), kind=kOutput, calls=%fused_computation.13 | convolution fusion | flops 201326592 | bytes 7340032 | tf_op jit(solution)/shard_map/oefj,efij->oei/dot_general | solution.py:40
  69.3 1.7 fusion.17
  71.0 14.1 %all_to_all.38 = f32[32,8,256]{2,0,1:T(8,128)S(1)} all-to-all(f32[32,8,256]{2,0,1:T(8,128)S(1)} %bitcast.138), channel_id=1, replica_groups=mesh['space'=64,'orb'=8] {'orb'}, dimensions={1} | all-to-all | bytes 524288 | tf_op jit(solution)/shard_map/all_to_all | solution.py:53
  85.1 1.1 fusion.49
  86.5 144.1 %all-reduce.4.cloned.1.call-done = f32[256,256]{0,1:T(8,128)} async-done(((f32[256,256]{0,1:T(8,128)}), f32[256,256]{0,1:T(8,128)}) %all-reduce.4.cloned.1.call-update) | async-done | bytes 262160 | tf_op jit(solution)/shard_map/psum | solution.py:57
  230.7 72.6 %all-reduce.6.cloned.1.call-done = f32[256,256]{0,1:T(8,128)} async-done(((f32[256,256]{0,1:T(8,128)}), f32[256,256]{0,1:T(8,128)}) %all-reduce.6.cloned.1.call-update) | async-done | bytes 262160 | tf_op jit(solution)/shard_map/psum | solution.py:57
  303.3 1.1 copy.40
  304.4 1.0 fusion.31
  305.4 11.7 %cholesky.50 = f32[128,128]{1,0:T(8,128)S(1)} custom-call(f32[128,128]{1,0:T(8,128)S(1)} %cholesky.118), custom_call_target="Cholesky" | custom-call | tf_op jit(solution)/shard_map/jit(cholesky)/cholesky | solution.py:58
  317.2 9.8 %custom-call.14 = f32[1,128,128]{1,2,0:T(8,128)S(1)} custom-call(f32[1,128,128]{2,1,0:T(8,128)S(1)} %get-tuple-element.34), custom_call_target="InvertDiagBlocksLowerTriangular" | custom-call | tf_op jit(solution)/shard_map/jit(cholesky)/cholesky | solution.py:58
  327.4 11.7 %cholesky.105 = f32[128,128]{1,0:T(8,128)S(1)} custom-call(f32[128,128]{1,0:T(8,128)S(1)} %convolution_subtract_fusion.1), custom_call_target="Cholesky" | custom-call | tf_op jit(solution)/shard_map/jit(cholesky)/cholesky | solution.py:58
  341.2 4.0 %while.1 = (s32[]{:T(128)}, f32[256,256]{1,0:T(8,128)S(1)}, s32[2,2]{1,0:T(2,128)S(1)}, f32[2,128,128]{2,1,0:T(8,128)S(1)}, s32[]{:T(128)}) while((s32[]{:T(128)}, f32[256,256]{1,0:T(8,128)S(1)}, s32[2,2]{1,0:T(2,128)S(1)}, f32[2,128,128]{2,1,0:T(8,128)S(1)}, s32[]{:T(128)}) %tuple.33), condition=%wide.while_cond, body=%wide.while_body.sunk | while | flops 2 | bytes 131181 | solution.py:59
  341.9 1.3 bitcast_dynamic-update-slice_fusion.2
  343.9 1.3 bitcast_dynamic-update-slice_fusion.2
  345.2 19.7 %custom-call.15 = f32[2,128,128]{1,2,0:T(8,128)S(1)} custom-call(f32[2,128,128]{2,1,0:T(8,128)S(1)} %get-tuple-element.10), custom_call_target="InvertDiagBlocksLowerTriangular" | custom-call | tf_op jit(solution)/shard_map/triangular_solve | solution.py:59
  366.5 5.4 %all-to-all-start.1 = ((f32[8,32,256]{2,1,0:T(8,128)}), f32[8,32,256]{2,1,0:T(8,128)S(1)}, u32[]{:S(2)}, u32[]{:S(2)}) async-start(f32[8,32,256]{2,1,0:T(8,128)} %bitcast.26), calls=%async_computation.1 | async-start | bytes 524288 | tf_op jit(solution)/shard_map/all_to_all | solution.py:60
  371.9 0.8 copy.42
  372.7 5.7 %all-to-all-done.1 = f32[8,32,256]{2,1,0:T(8,128)S(1)} async-done(((f32[8,32,256]{2,1,0:T(8,128)}), f32[8,32,256]{2,1,0:T(8,128)S(1)}, u32[]{:S(2)}, u32[]{:S(2)}) %all-to-all-start.1) | async-done | bytes 262176 | tf_op jit(solution)/shard_map/all_to_all | solution.py:60
  (53 shorter events, 10.2 us)
Async XLA Ops:
  7.2 25.3 %copy-start = (bf16[32,2048]{1,0:T(8,128)(2,1)S(1)}, bf16[32,2048]{1,0:T(8,128)(2,1)}, u32[]{:S(2)}) copy-start(bf16[32,2048]{1,0:T(8,128)(2,1)} %param.6) | copy-start | bytes 393220
  7.2 223.4 %all-reduce.4.cloned.1.call-start = ((), (), s32[]{:S(2)}) async-start(), calls=%async_computation.2 | async-start | bytes 524288 | tf_op jit(solution)/shard_map/psum | solution.py:57
  7.2 17.8 %collective-permute-start = (bf16[32,2048]{1,0:T(8,128)(2,1)}, bf16[32,2048]{1,0:T(8,128)(2,1)S(1)}, u32[]{:S(2)}, u32[]{:S(2)}) collective-permute-start(bf16[32,2048]{1,0:T(8,128)(2,1)} %param.6), channel_id=1, source_target_pairs={{0,8},{8,16},{16,24},{24,32},{32,40},{40,48},{48,56},{56,64},{64,7... | collective-permute-start | bytes 393224 | tf_op jit(solution)/shard_map/ppermute | solution.py:16
  12.0 14.0 %collective-permute-start.1 = (bf16[32,2048]{1,0:T(8,128)(2,1)}, bf16[32,2048]{1,0:T(8,128)(2,1)S(1)}, u32[]{:S(2)}, u32[]{:S(2)}) collective-permute-start(bf16[32,2048]{1,0:T(8,128)(2,1)} %param.6), channel_id=1, source_target_pairs={{8,0},{16,8},{24,16},{32,24},{40,32},{48,40},{56,48},{64,56},{72,6... | collective-permute-start | bytes 393224 | tf_op jit(solution)/shard_map/ppermute | solution.py:19
  34.2 9.7 %collective-permute-start.2 = (bf16[32,2048]{1,0:T(8,128)(2,1)S(1)}, bf16[32,2048]{1,0:T(8,128)(2,1)S(1)}, u32[]{:S(2)}, u32[]{:S(2)}) collective-permute-start(bf16[32,2048]{1,0:T(8,128)(2,1)S(1)} %fusion.27), channel_id=1, source_target_pairs={{0,8},{8,16},{16,24},{24,32},{32,40},{40,48},{48,56},{56,64},{64,7... | collective-permute-start | bytes 393224 | tf_op jit(solution)/shard_map/ppermute | solution.py:16
  36.2 9.3 %collective-permute-start.3 = (bf16[32,2048]{1,0:T(8,128)(2,1)S(1)}, bf16[32,2048]{1,0:T(8,128)(2,1)S(1)}, u32[]{:S(2)}, u32[]{:S(2)}) collective-permute-start(bf16[32,2048]{1,0:T(8,128)(2,1)S(1)} %fusion.27), channel_id=1, source_target_pairs={{8,0},{16,8},{24,16},{32,24},{40,32},{48,40},{56,48},{64,56},{72,6... | collective-permute-start | bytes 393224 | tf_op jit(solution)/shard_map/ppermute | solution.py:19
  52.7 9.4 %collective-permute-start.4 = (bf16[32,2048]{1,0:T(8,128)(2,1)S(1)}, bf16[32,2048]{1,0:T(8,128)(2,1)S(1)}, u32[]{:S(2)}, u32[]{:S(2)}) collective-permute-start(bf16[32,2048]{1,0:T(8,128)(2,1)S(1)} %fusion.28), channel_id=1, source_target_pairs={{0,8},{8,16},{16,24},{24,32},{32,40},{40,48},{48,56},{56,64},{64,7... | collective-permute-start | bytes 393224 | tf_op jit(solution)/shard_map/ppermute | solution.py:16
  54.7 9.0 %collective-permute-start.5 = (bf16[32,2048]{1,0:T(8,128)(2,1)S(1)}, bf16[32,2048]{1,0:T(8,128)(2,1)S(1)}, u32[]{:S(2)}, u32[]{:S(2)}) collective-permute-start(bf16[32,2048]{1,0:T(8,128)(2,1)S(1)} %fusion.28), channel_id=1, source_target_pairs={{8,0},{16,8},{24,16},{32,24},{40,32},{48,40},{56,48},{64,56},{72,6... | collective-permute-start | bytes 393224 | tf_op jit(solution)/shard_map/ppermute | solution.py:19
  86.3 217.0 %all-reduce.6.cloned.1.call-start = ((), (), s32[]{:S(2)}) async-start(), calls=%async_computation.3 | async-start | bytes 524288 | tf_op jit(solution)/shard_map/psum | solution.py:57
  366.5 11.9 %all-to-all-start.1 = ((f32[8,32,256]{2,1,0:T(8,128)}), f32[8,32,256]{2,1,0:T(8,128)S(1)}, u32[]{:S(2)}, u32[]{:S(2)}) async-start(f32[8,32,256]{2,1,0:T(8,128)} %bitcast.26), calls=%async_computation.1 | async-start | bytes 524288 | tf_op jit(solution)/shard_map/all_to_all | solution.py:60
Sparse Core Ops, SparseCore 0:
  86.4 144.1 all-reduce.3
  232.9 70.3 all-reduce.5
